TPU v7x, 32 devices: a whole 2x2x4 slice. The times are simulated.
32 devices in a mesh: seq: 8 (over y, x, core), dp: 4 (over z).
Axes of the slice: x: 2, y: 2, z: 4, core: 2. Of those that a mesh axis runs over, the one named last changes fastest.
Arguments:
- query: bfloat16 [4, 1536, 1280], P('dp', 'seq'), may hold values from -52 to 52, as said below
- keys: bfloat16 [4, 1536, 1280], P('dp', 'seq'), may hold values from -6 to 6, as said below
- values: bfloat16 [4, 1536, 1280], P('dp', 'seq'), may hold values from -6 to 6
- attn: bfloat16 [4, 1536, 1280], P('dp', 'seq'), may hold values from -6 to 6
- d_block: bfloat16 [4, 1536, 1280], P('dp', 'seq'), may hold values from -6 to 6
- w_out: bfloat16 [1280, 1280], P('dp'), may hold values from -0.15625 to 0.15625
Outputs:
- d_query: bfloat16 [4, 1536, 1280], P('dp', 'seq')
- d_keys: bfloat16 [4, 1536, 1280], P('dp', 'seq')
- d_values: bfloat16 [4, 1536, 1280], P('dp', 'seq')
- d_weight: float32 [1280, 1280], P('dp')
Inputs may be any that keep to these rules, and one draw needn't show every extreme that they name: Some query patches may lie along the sum of two keys of the same video. keys has entries of order one.
All inputs are finite; a program needn't handle non-finite values.
Results may differ from a plain program's by a relative error of at most 0.0058.
Values may be sent and summed in bfloat16 or wider, within the bound.
A program may use at most 64 MiB of HBM per device.

v0:
```python
import functools
import math

import jax
import jax.numpy as jnp
from jax import lax
from jax.experimental import pallas as pl
from jax.experimental.pallas import tpu as pltpu
from jax.sharding import PartitionSpec as P

HEAD_DIM = 80
LANES = 128
MESH = pl.DeviceIdType.MESH
VMEM_LIMIT = 60 * 1024 * 1024
LAST = (((1,), (1,)), ((), ()))
FIRST = (((0,), (0,)), ((), ()))


def gather_kernel(
    seq, dp, q_ref, k_ref, v_ref, a_ref, g_ref, w_ref, pack_out, g_out, w_out,
    packed, g_send, g_recv, f_send, w_send, w_recv, p_send, p_recv, local_sem,
):
    s = lax.axis_index("seq")
    d = lax.axis_index("dp")
    ratio = seq // dp
    home = s // ratio
    partner = s + 1 - 2 * (s % 2)
    width = k_ref.shape[1] // seq

    barrier = pltpu.get_barrier_semaphore()
    for step in range(1, seq):
        pl.semaphore_signal(barrier, inc=1, device_id=(lax.rem(s + step, seq), d), device_id_type=MESH)
    for step in range(1, dp):
        pl.semaphore_signal(barrier, inc=1, device_id=(s, lax.rem(d + step, dp)), device_id_type=MESH)
    pl.semaphore_wait(barrier, seq + dp - 2)

    def w_copy(step):
        return pltpu.make_async_remote_copy(
            src_ref=w_ref.at[s % ratio],
            dst_ref=w_out,
            send_sem=w_send.at[step],
            recv_sem=w_recv,
            device_id=(s, lax.rem(d + step, dp)),
            device_id_type=MESH,
        )

    def direct(step):
        return pltpu.make_async_remote_copy(
            src_ref=g_ref,
            dst_ref=g_out.at[s],
            send_sem=g_send.at[step],
            recv_sem=g_recv.at[s],
            device_id=(lax.rem(s + 2 * step, seq), d),
            device_id_type=MESH,
        )

    def forward(step):
        source = lax.rem(s + seq - 2 * step, seq)
        return pltpu.make_async_remote_copy(
            src_ref=g_ref if step == 0 else g_out.at[source],
            dst_ref=g_out.at[source],
            send_sem=f_send.at[step],
            recv_sem=g_recv.at[source],
            device_id=(partner, d),
            device_id_type=MESH,
        )

    def arrived(source):
        pltpu.make_async_remote_copy(
            src_ref=g_ref,
            dst_ref=g_out.at[source],
            send_sem=f_send.at[0],
            recv_sem=g_recv.at[source],
            device_id=(partner, d),
            device_id_type=MESH,
        ).wait_recv()

    def pack_copy(step):
        peer = lax.rem(s + step, seq)
        return pltpu.make_async_remote_copy(
            src_ref=packed.at[peer],
            dst_ref=pack_out.at[s],
            send_sem=p_send.at[step],
            recv_sem=p_recv.at[s],
            device_id=(peer, d),
            device_id_type=MESH,
        )

    own_g = pltpu.make_async_copy(g_ref, g_out.at[s], local_sem.at[0])
    own_w = pltpu.make_async_copy(w_ref.at[s % ratio], w_out, local_sem.at[1])
    own_pack = pltpu.make_async_copy(packed.at[s], pack_out.at[s], local_sem.at[2])

    for step in range(1, seq // 2):
        direct(step).start()
    forward(0).start()
    own_g.start()

    @pl.when(home == d)
    def _():
        for step in range(1, dp):
            w_copy(step).start()
        own_w.start()

    for peer in range(seq):
        for index, ref in enumerate((q_ref, k_ref, v_ref, a_ref)):
            packed[peer, :, index * width : (index + 1) * width] = ref[
                :, peer * width : (peer + 1) * width
            ]
    for step in range(1, seq):
        pack_copy(step).start()
    own_pack.start()

    for step in range(1, seq // 2):
        arrived(lax.rem(s + seq - 2 * step, seq))
        forward(step).start()
    for step in range(seq // 2):
        arrived(lax.rem(partner + seq - 2 * step, seq))
    for step in range(1, seq):
        source = lax.rem(s + seq - step, seq)
        pltpu.make_async_remote_copy(
            src_ref=packed.at[source],
            dst_ref=pack_out.at[source],
            send_sem=p_send.at[step],
            recv_sem=p_recv.at[source],
            device_id=(source, d),
            device_id_type=MESH,
        ).wait_recv()

    @pl.when(home == d)
    def _():
        for step in range(1, dp):
            w_copy(step).wait_send()
        own_w.wait()

    @pl.when(home != d)
    def _():
        w_copy(1).wait_recv()

    own_g.wait()
    own_pack.wait()
    for step in range(1, seq // 2):
        direct(step).wait_send()
    for step in range(seq // 2):
        forward(step).wait_send()
    for step in range(1, seq):
        pack_copy(step).wait_send()


def gather(seq, dp, query, keys, values, attn, grad_y, w_rows):
    rows, features = query.shape
    width = features // seq
    dma = pltpu.SemaphoreType.DMA
    vmem = pl.BlockSpec(memory_space=pltpu.VMEM)
    hbm = pl.BlockSpec(memory_space=pl.ANY)
    return pl.pallas_call(
        functools.partial(gather_kernel, seq, dp),
        out_shape=(
            jax.ShapeDtypeStruct((seq, rows, 4 * width), jnp.bfloat16),
            jax.ShapeDtypeStruct((seq, rows, features), jnp.bfloat16),
            jax.ShapeDtypeStruct((width, features), jnp.bfloat16),
        ),
        in_specs=[vmem] * 6,
        out_specs=(hbm, hbm, hbm),
        scratch_shapes=[
            pltpu.VMEM((seq, rows, 4 * width), jnp.bfloat16),
            dma((seq,)),
            dma((seq,)),
            dma((seq,)),
            dma((dp,)),
            dma(()),
            dma((seq,)),
            dma((seq,)),
            dma((3,)),
        ],
        compiler_params=pltpu.CompilerParams(
            collective_id=0, has_side_effects=True, vmem_limit_bytes=VMEM_LIMIT
        ),
        name="gather_heads",
    )(query, keys, values, attn, grad_y, w_rows)


def backward_kernel(
    seq, dp, heads, block_rows, factor, pack_ref, g_ref, w_ref, landed, spread,
    q_s, k_s, v_s, do_s, delta_s, dk_s, dv_s, grad_s, dw_s, middle, parts, total_s,
    p_send, p_recv, w_send, w_recv, z_send, z_recv, t_send, f_send, t_recv, local_sem,
):
    s = lax.axis_index("seq")
    d = lax.axis_index("dp")
    ratio = seq // dp
    partner = s + 1 - 2 * (s % 2)
    patches = pack_ref.shape[0]
    rows_here = patches // seq
    width = heads * HEAD_DIM
    scale = HEAD_DIM ** (-0.5)
    to_log2 = scale * math.log2(math.e)

    def w_copy(peer, source):
        return pltpu.make_async_remote_copy(
            src_ref=dw_s.at[peer],
            dst_ref=middle.at[source],
            send_sem=w_send.at[peer],
            recv_sem=w_recv.at[source],
            device_id=(peer, d),
            device_id_type=MESH,
        )

    def z_copy(plane, source):
        return pltpu.make_async_remote_copy(
            src_ref=middle.at[pl.ds(plane * ratio, ratio)],
            dst_ref=parts.at[source],
            send_sem=z_send.at[plane],
            recv_sem=z_recv.at[source],
            device_id=(s, plane),
            device_id_type=MESH,
        )

    def grad_copy(h, peer, source):
        start = pl.multiple_of(peer * rows_here, rows_here)
        return pltpu.make_async_remote_copy(
            src_ref=grad_s.at[h, pl.ds(start, rows_here)],
            dst_ref=landed.at[h, source],
            send_sem=p_send.at[h, peer],
            recv_sem=p_recv.at[h, source],
            device_id=(peer, d),
            device_id_type=MESH,
        )

    def own_grad(h):
        start = pl.multiple_of(s * rows_here, rows_here)
        return pltpu.make_async_copy(
            grad_s.at[h, pl.ds(start, rows_here)], landed.at[h, s], local_sem.at[2 + h]
        )

    def direct(step):
        return pltpu.make_async_remote_copy(
            src_ref=total_s,
            dst_ref=spread.at[s],
            send_sem=t_send.at[step],
            recv_sem=t_recv.at[s],
            device_id=(lax.rem(s + 2 * step, seq), d),
            device_id_type=MESH,
        )

    def forward(step):
        source = lax.rem(s + seq - 2 * step, seq)
        return pltpu.make_async_remote_copy(
            src_ref=total_s if step == 0 else spread.at[source],
            dst_ref=spread.at[source],
            send_sem=f_send.at[step],
            recv_sem=t_recv.at[source],
            device_id=(partner, d),
            device_id_type=MESH,
        )

    def arrived(source):
        pltpu.make_async_remote_copy(
            src_ref=total_s,
            dst_ref=spread.at[source],
            send_sem=f_send.at[0],
            recv_sem=t_recv.at[source],
            device_id=(partner, d),
            device_id_type=MESH,
        ).wait_recv()

    own_middle = pltpu.make_async_copy(dw_s.at[s], middle.at[s], local_sem.at[0])
    own_part = pltpu.make_async_copy(
        middle.at[pl.ds(d * ratio, ratio)], parts.at[d], local_sem.at[2 + heads]
    )
    own_total = pltpu.make_async_copy(total_s, spread.at[s], local_sem.at[1])

    barrier = pltpu.get_barrier_semaphore()
    for step in range(1, seq):
        pl.semaphore_signal(barrier, inc=1, device_id=(lax.rem(s + step, seq), d), device_id_type=MESH)
    for step in range(1, dp):
        pl.semaphore_signal(barrier, inc=1, device_id=(s, lax.rem(d + step, dp)), device_id_type=MESH)

    piece = width // seq
    groups = g_ref.shape[1] // LANES
    used = piece * groups
    d_weight = lax.dot_general(
        pack_ref[:, 3 * width : 4 * width], g_ref[...], FIRST, preferred_element_type=jnp.float32
    )
    d_weight = d_weight * factor
    for index in range(seq):
        share = d_weight[index * piece : (index + 1) * piece, :]
        tall = [share[:, group * LANES : (group + 1) * LANES] for group in range(groups)]
        tall.append(jnp.zeros((dw_s.shape[1] - used, LANES), jnp.float32))
        dw_s[index] = jnp.concatenate(tall, axis=0).astype(jnp.bfloat16)

    pl.semaphore_wait(barrier, seq + dp - 2)
    for step in range(1, seq):
        w_copy(lax.rem(s + step, seq), s).start()
    own_middle.start()

    def relay():
        own_middle.wait()
        for step in range(1, seq):
            source = lax.rem(s + seq - step, seq)
            w_copy(source, source).wait_recv()
        for step in range(1, dp):
            z_copy(lax.rem(d + step, dp), d).start()
        own_part.start()

    def combine():
        own_part.wait()
        for step in range(1, dp):
            source = lax.rem(d + dp - step, dp)
            z_copy(source, source).wait_recv()
        for column in range(ratio):
            value = parts[0, column].astype(jnp.float32)
            for plane in range(1, dp):
                value = value + parts[plane, column].astype(jnp.float32)
            total_s[column] = value.astype(jnp.bfloat16)
        for step in range(1, seq // 2):
            direct(step).start()
        forward(0).start()
        own_total.start()

    @pl.loop(0, patches // block_rows)
    def _(block):
        rows = pl.ds(pl.multiple_of(block * block_rows, block_rows), block_rows)
        d_out = lax.dot_general(
            g_ref[rows, :], w_ref[...], LAST, preferred_element_type=jnp.float32
        ).astype(jnp.bfloat16)
        for h in range(heads):
            low = h * HEAD_DIM
            q_s[h, rows, :] = pack_ref[rows, low : low + HEAD_DIM]
            k_s[h, rows, :] = pack_ref[rows, width + low : width + low + HEAD_DIM]
            v_s[h, rows, :] = pack_ref[rows, 2 * width + low : 2 * width + low + HEAD_DIM]
            a_h = pack_ref[rows, 3 * width + low : 3 * width + low + HEAD_DIM]
            do_h = d_out[:, low : low + HEAD_DIM]
            do_s[h, rows, :] = do_h
            product = do_h.astype(jnp.float32) * a_h.astype(jnp.float32)
            delta_s[h, block] = jnp.sum(product.T, axis=0, keepdims=True)

    blocks = patches // block_rows
    for h in range(heads):
        dk_s[...] = jnp.zeros_like(dk_s)
        dv_s[...] = jnp.zeros_like(dv_s)

        @pl.loop(0, patches // block_rows)
        def _(block):
            rows = pl.ds(pl.multiple_of(block * block_rows, block_rows), block_rows)
            if h == 0:
                pl.when(block == min(1, blocks - 1))(relay)
            if h == heads - 1:
                pl.when(block == min(1 if heads > 1 else 2, blocks - 1))(combine)
            q_b = q_s[h, rows, :]
            do_b = do_s[h, rows, :]
            keys = k_s[h]
            scores = lax.dot_general(keys, q_b, LAST, preferred_element_type=jnp.float32)
            top = jnp.max(scores, axis=0, keepdims=True)
            exps = jnp.exp2((scores - top) * to_log2)
            probs = exps * (1.0 / jnp.sum(exps, axis=0, keepdims=True))
            d_probs = lax.dot_general(v_s[h], do_b, LAST, preferred_element_type=jnp.float32)
            d_scores = (probs * (d_probs - delta_s[h, block]) * scale).astype(jnp.bfloat16)
            dv_s[...] += jnp.dot(probs.astype(jnp.bfloat16), do_b, preferred_element_type=jnp.float32)
            dk_s[...] += jnp.dot(d_scores, q_b, preferred_element_type=jnp.float32)
            dq_t = lax.dot_general(keys, d_scores, FIRST, preferred_element_type=jnp.float32)
            grad_s[h, rows, 0:HEAD_DIM] = dq_t.T.astype(jnp.bfloat16)

        grad_s[h, :, HEAD_DIM : 2 * HEAD_DIM] = dk_s[...].astype(jnp.bfloat16)
        grad_s[h, :, 2 * HEAD_DIM : 3 * HEAD_DIM] = dv_s[...].astype(jnp.bfloat16)

        for step in range(1, seq):
            grad_copy(h, lax.rem(s + step, seq), s).start()
        own_grad(h).start()

    for step in range(1, seq // 2):
        arrived(lax.rem(s + seq - 2 * step, seq))
        forward(step).start()
    for h in range(heads):
        own_grad(h).wait()
        for step in range(1, seq):
            source = lax.rem(s + seq - step, seq)
            grad_copy(h, source, source).wait_recv()
    for step in range(seq // 2):
        arrived(lax.rem(partner + seq - 2 * step, seq))

    own_total.wait()
    for step in range(1, seq):
        w_copy(lax.rem(s + step, seq), s).wait_send()
    for step in range(1, dp):
        z_copy(lax.rem(d + step, dp), d).wait_send()

    for step in range(1, seq):
        for h in range(heads):
            grad_copy(h, lax.rem(s + step, seq), s).wait_send()
    for step in range(1, seq // 2):
        direct(step).wait_send()
    for step in range(seq // 2):
        forward(step).wait_send()


def backward(seq, dp, factor, packed, grad_y, w_rows):
    total = packed.shape[0]
    width, features = w_rows.shape
    heads = width // HEAD_DIM
    ratio = seq // dp
    tall = -(-(width // seq * features // LANES) // 16) * 16
    block_rows = 768
    while total % block_rows:
        block_rows //= 2
    dma = pltpu.SemaphoreType.DMA
    vmem = pl.BlockSpec(memory_space=pltpu.VMEM)
    hbm = pl.BlockSpec(memory_space=pl.ANY)
    low = pltpu.VMEM((heads, total, HEAD_DIM), jnp.bfloat16)
    wide = pltpu.VMEM((total, HEAD_DIM), jnp.float32)
    return pl.pallas_call(
        functools.partial(backward_kernel, seq, dp, heads, block_rows, factor),
        out_shape=(
            jax.ShapeDtypeStruct((heads, seq, total // seq, 3 * HEAD_DIM), jnp.bfloat16),
            jax.ShapeDtypeStruct((seq, ratio, tall, LANES), jnp.bfloat16),
        ),
        in_specs=[vmem] * 3,
        out_specs=(hbm, hbm),
        scratch_shapes=[
            low, low, low, low,
            pltpu.VMEM((heads, total // block_rows, 1, block_rows), jnp.float32),
            wide, wide,
            pltpu.VMEM((heads, total, 3 * HEAD_DIM), jnp.bfloat16),
            pltpu.VMEM((seq, tall, LANES), jnp.bfloat16),
            pltpu.VMEM((seq, tall, LANES), jnp.bfloat16),
            pltpu.VMEM((dp, ratio, tall, LANES), jnp.bfloat16),
            pltpu.VMEM((ratio, tall, LANES), jnp.bfloat16),
            dma((heads, seq)),
            dma((heads, seq)),
            dma((seq,)),
            dma((seq,)),
            dma((dp,)),
            dma((dp,)),
            dma((seq,)),
            dma((seq,)),
            dma((seq,)),
            dma((3 + heads,)),
        ],
        compiler_params=pltpu.CompilerParams(
            collective_id=1, has_side_effects=True, vmem_limit_bytes=VMEM_LIMIT
        ),
        name="attention_backward",
    )(packed, grad_y, w_rows)


def unpack_kernel(landed, spread, dq_ref, dk_ref, dv_ref, out_ref):
    heads, seq = landed.shape[:2]
    ratio = spread.shape[1]
    width = heads * HEAD_DIM
    piece = width // seq
    groups = out_ref.shape[1] // LANES
    for source in range(seq):
        for h in range(heads):
            start = source * width + h * HEAD_DIM
            for index, ref in enumerate((dq_ref, dk_ref, dv_ref)):
                ref[:, start : start + HEAD_DIM] = landed[
                    h, source, :, index * HEAD_DIM : (index + 1) * HEAD_DIM
                ]
        for column in range(ratio):
            start = column * width + source * piece
            tall = spread[source, column].astype(jnp.float32)
            for group in range(groups):
                out_ref[start : start + piece, group * LANES : (group + 1) * LANES] = tall[
                    group * piece : (group + 1) * piece
                ]


def unpack(dp, landed, spread):
    rows = landed.shape[2]
    features = landed.shape[0] * landed.shape[1] * HEAD_DIM
    vmem = pl.BlockSpec(memory_space=pltpu.VMEM)
    block = jax.ShapeDtypeStruct((rows, features), jnp.bfloat16)
    return pl.pallas_call(
        unpack_kernel,
        out_shape=(
            block, block, block,
            jax.ShapeDtypeStruct((features // dp, features), jnp.float32),
        ),
        in_specs=[vmem] * 2,
        out_specs=(vmem,) * 4,
        compiler_params=pltpu.CompilerParams(vmem_limit_bytes=VMEM_LIMIT),
        name="unpack",
    )(landed, spread)


def body(query, keys, values, attn, d_block, w_out):
    seq = lax.axis_size("seq")
    dp = lax.axis_size("dp")
    rows, features = query.shape[1:]
    width = features // seq
    flat = lambda array: array.reshape(rows, features)
    packed, grad_y, w_rows = gather(
        seq, dp, flat(query), flat(keys), flat(values), flat(attn), flat(d_block),
        w_out.reshape(seq // dp, width, features),
    )
    factor = 1.0 / float(dp * rows * seq) ** 0.5
    landed, spread = backward(
        seq, dp, factor,
        packed.reshape(seq * rows, 4 * width),
        grad_y.reshape(seq * rows, features),
        w_rows,
    )
    d_query, d_keys, d_values, d_weight = unpack(dp, landed, spread)
    whole = lambda array: array.reshape(1, rows, features)
    return whole(d_query), whole(d_keys), whole(d_values), d_weight


def solution(mesh):
    blocks = P("dp", "seq", None)
    return jax.shard_map(
        body,
        mesh=mesh,
        in_specs=(blocks,) * 5 + (P("dp", None),),
        out_specs=(blocks, blocks, blocks, P("dp", None)),
        check_vma=False,
    )
```

profile of v0, /device:TPU:1, one launch (start us, length us, event | category | flops | bytes accessed | tf_op | source)
XLA Modules:
  0.0 96.1 jit_solution(16685886886405494058)
XLA Ops:
  0.6 51.0 %gather_heads.1 = (bf16[8,192,640]{2,1,0:T(8,128)(2,1)}, bf16[8,192,1280]{2,1,0:T(8,128)(2,1)}, bf16[160,1280]{1,0:T(8,128)(2,1)}) custom-call(bf16[192,1280]{1,0:T(8,128)(2,1)} %bitcast.14, bf16[192,1280]{1,0:T(8,128)(2,1)} %bitcast.15, bf16[192,1280]{1,0:T(8,128)(2,1)} %bitcast.16, bf16[192,1280]{1,0:T(8,128)(2,1)} %bitcast.17, ...), custom_call_target="tpu_custom_call" | custom-call | tf_op jit(solution)/shard_map/gather_heads/pallas_call | solution.py:155
  51.6 40.1 %attention_backward.1 = (bf16[2,8,192,240]{3,2,1,0:T(8,128)(2,1)}, bf16[8,2,208,128]{3,2,1,0:T(8,128)(2,1)}) custom-call(bf16[1536,640]{1,0:T(8,128)(2,1)} %bitcast.12, bf16[1536,1280]{1,0:T(8,128)(2,1)} %bitcast.11, bf16[160,1280]{1,0:T(8,128)(2,1)} %get-tuple-element.15.w_ref), custom_call_target="tpu_custom_call" | custom-call | tf_op jit(solution)/shard_map/attention_backward/pallas_call | solution.py:409
  91.7 4.4 %unpack.1 = (bf16[192,1280]{1,0:T(8,128)(2,1)}, bf16[192,1280]{1,0:T(8,128)(2,1)}, bf16[192,1280]{1,0:T(8,128)(2,1)}, f32[320,1280]{1,0:T(8,128)}) custom-call(bf16[2,8,192,240]{3,2,1,0:T(8,128)(2,1)} %get-tuple-element.16.landed, bf16[8,2,208,128]{3,2,1,0:T(8,128)(2,1)} %get-tuple-element.17.spread), custom_call_target="tpu_custom_call" | custom-call | tf_op jit(solution)/shard_map/unpack/pallas_call | solution.py:471
where the time goes:
time: 96.2 us; the launch traced here: 96.1 us
  Pallas kernels  95.4 us (99%)
    pallas_call x1, Pallas kernels, gather(): pl.pallas_call(functools.partial(gather_kernel, seq, dp), out_shape=(jax....  51 us
    pallas_call x1, Pallas kernels, backward(): pl.pallas_call(functools.partial(backward_kernel, seq, dp, heads, block_r...  40.1 us
    pallas_call x1, Pallas kernels, unpack(): pl.pallas_call(unpack_kernel, out_shape=(block, block, block, jax.ShapeDt...  4.36 us

commit v1 on v0

v1 whole, which is shorter than its diff:
```python
import functools
import math

import jax
import jax.numpy as jnp
from jax import lax
from jax.experimental import pallas as pl
from jax.experimental.pallas import tpu as pltpu
from jax.sharding import PartitionSpec as P

HEAD_DIM = 80
AUG = HEAD_DIM + 8
MESH = pl.DeviceIdType.MESH
VMEM_LIMIT = 62 * 1024 * 1024
LAST = (((1,), (1,)), ((), ()))
FIRST = (((0,), (0,)), ((), ()))
BF16 = jnp.bfloat16
F32 = jnp.float32


def attention_kernel(
    seq, dp, heads, block, factor,
    q_hbm, k_hbm, v_hbm, a_hbm, g_hbm, w_hbm, landed, spread,
    q_v, k_v, v_v, g_v, a2, g2, w_all, packed, pack_in, do_out, do_in,
    q_s, k_s, v_s, qs_s, dos_s, e_s, inv_s, dqt_s, grad_s,
    p_s, up_out, up_in, dn_out, dn_in, acc_s, rs_out, rs_in, total_s,
    in_sem, own_sem, wu_send, wd_send, wp_send, w_recv, x_send, x_recv,
    q_send, q_recv, do_send, do_recv, g_send, g_recv,
    up_send, up_recv, dn_send, dn_recv, rs_send, rs_recv, t_send, f_send, t_recv,
):
    s = lax.axis_index("seq")
    d = lax.axis_index("dp")
    core = s % 2
    chip = s // 2
    chips = seq // 2
    partner = s + 1 - 2 * core
    ratio = seq // dp
    rows, features = q_v.shape
    half = features // 2
    width = heads * HEAD_DIM
    patches = seq * rows
    slab = features // dp
    share = slab // chips
    blocks = patches // block
    scale = HEAD_DIM ** (-0.5)
    to_log2 = scale * math.log2(math.e)

    def columns(which):
        return pl.ds(pl.multiple_of(which * half, 128), half)

    def remote(src, dst, send, recv, peer, plane):
        return pltpu.make_async_remote_copy(
            src_ref=src, dst_ref=dst, send_sem=send, recv_sem=recv,
            device_id=(peer, plane), device_id_type=MESH,
        )

    barrier = pltpu.get_barrier_semaphore()
    for step in range(1, seq):
        pl.semaphore_signal(barrier, inc=1, device_id=(lax.rem(s + step, seq), d), device_id_type=MESH)
    for step in range(1, dp):
        pl.semaphore_signal(barrier, inc=1, device_id=(s, lax.rem(d + step, dp)), device_id_type=MESH)

    loads = [
        pltpu.make_async_copy(src, dst, in_sem.at[index])
        for index, (src, dst) in enumerate((
            (q_hbm, q_v), (k_hbm, k_v), (v_hbm, v_v), (a_hbm, a2.at[0]), (g_hbm, g_v),
            (g_hbm.at[:, columns(core)], g2.at[0]),
        ))
    ]
    own_w = [
        pltpu.make_async_copy(
            w_hbm.at[:, h], w_all.at[h, pl.ds(d * ratio, ratio)], in_sem.at[6 + h]
        )
        for h in range(heads)
    ]
    for copy in loads + own_w:
        copy.start()

    def w_piece(h, b, which):
        return w_all.at[h, pl.ds(b * ratio, ratio), :, columns(which)]

    def w_up(h, b, own):
        src = w_hbm.at[:, h, :, columns(core)] if own else w_piece(h, b, core)
        return remote(src, w_piece(h, b, core), wu_send.at[h, b], w_recv.at[h, b, core], s, d + 1)

    def w_down(h, b, own):
        src = w_hbm.at[:, h, :, columns(core)] if own else w_piece(h, b, core)
        return remote(src, w_piece(h, b, core), wd_send.at[h, b], w_recv.at[h, b, core], s, d - 1)

    def w_side(h, b, which):
        return remote(
            w_piece(h, b, which), w_piece(h, b, which), wp_send.at[h, b], w_recv.at[h, b, which], partner, d
        )

    def w_own(h):
        pl.when(d < dp - 1)(lambda: w_up(h, d, True).start())
        pl.when(d > 0)(lambda: w_down(h, d, True).start())

    def w_relay(h, dist):
        @pl.when(d >= dist)
        def _():
            b = d - dist
            w_side(h, b, core).wait_recv()
            pl.when(d < dp - 1)(lambda: w_up(h, b, False).start())
            w_side(h, b, core).start()

        @pl.when(d + dist < dp)
        def _():
            b = d + dist
            w_side(h, b, core).wait_recv()
            pl.when(d > 0)(lambda: w_down(h, b, False).start())
            w_side(h, b, core).start()

    def w_finish(h):
        for dist in range(1, dp):
            pl.when(d >= dist)(lambda: w_side(h, d - dist, 1 - core).wait_recv())
            pl.when(d + dist < dp)(lambda: w_side(h, d + dist, 1 - core).wait_recv())
        own_w[h].wait()

    def w_drain(h):
        pl.when(d < dp - 1)(lambda: w_up(h, d, True).wait_send())
        pl.when(d > 0)(lambda: w_down(h, d, True).wait_send())
        for dist in range(1, dp):
            @pl.when(d >= dist)
            def _():
                pl.when(d < dp - 1)(lambda: w_up(h, d - dist, False).wait_send())
                w_side(h, d - dist, core).wait_send()

            @pl.when(d + dist < dp)
            def _():
                pl.when(d > 0)(lambda: w_down(h, d + dist, False).wait_send())
                w_side(h, d + dist, core).wait_send()

    def q_copy(h, peer, source):
        return remote(packed.at[h, peer], pack_in.at[h, source], q_send.at[h, peer], q_recv.at[h, source], peer, d)

    def do_copy(h, peer, source):
        return remote(do_out.at[h, peer], do_in.at[h, source], do_send.at[h, peer], do_recv.at[h, source], peer, d)

    def grad_copy(h, peer, source):
        start = pl.multiple_of(peer * rows, rows)
        return remote(
            grad_s.at[h, pl.ds(start, rows)], landed.at[h, source], g_send.at[h, peer], g_recv.at[h, source], peer, d
        )

    def own_q(h):
        return pltpu.make_async_copy(packed.at[h, s], pack_in.at[h, s], own_sem.at[0, h])

    def own_do(h):
        return pltpu.make_async_copy(do_out.at[h, s], do_in.at[h, s], own_sem.at[1, h])

    def own_grad(h):
        start = pl.multiple_of(s * rows, rows)
        return pltpu.make_async_copy(grad_s.at[h, pl.ds(start, rows)], landed.at[h, s], own_sem.at[2, h])

    def send_all(copy, own, h):
        for step in range(1, seq):
            copy(h, lax.rem(s + step, seq), s).start()
        own(h).start()

    def await_all(copy, own, h):
        own(h).wait()
        for step in range(1, seq):
            source = lax.rem(s + seq - step, seq)
            copy(h, source, source).wait_recv()

    def drain_all(copy, h):
        for step in range(1, seq):
            copy(h, lax.rem(s + step, seq), s).wait_send()

    def pack(h):
        for peer in range(seq):
            low = peer * width + h * HEAD_DIM
            for index, ref in enumerate((q_v, k_v, v_v)):
                packed[h, peer, :, index * HEAD_DIM : (index + 1) * HEAD_DIM] = ref[:, low : low + HEAD_DIM]

    def make_d_out(h):
        d_out = lax.dot_general(
            g_v[...], w_all[h].reshape(seq * HEAD_DIM, features), LAST, preferred_element_type=F32
        ).astype(BF16)
        lane = lax.broadcasted_iota(jnp.int32, (rows, AUG - HEAD_DIM), 1)
        for peer in range(seq):
            low = peer * width + h * HEAD_DIM
            piece = d_out[:, peer * HEAD_DIM : (peer + 1) * HEAD_DIM]
            product = piece.astype(F32) * a2[0, :, low : low + HEAD_DIM].astype(F32)
            minus = -jnp.sum(product, axis=1, keepdims=True)
            first = minus.astype(BF16).astype(F32)
            second = (minus - first).astype(BF16).astype(F32)
            third = minus - first - second
            tail = jnp.where(lane == 0, first, jnp.where(lane == 1, second, jnp.where(lane == 2, third, 0.0)))
            do_out[h, peer, :, 0:HEAD_DIM] = piece
            do_out[h, peer, :, HEAD_DIM:AUG] = tail.astype(BF16)

    def a_swap():
        return remote(a_hbm, a2.at[1], x_send.at[0], x_recv.at[0], partner, d)

    def g_swap():
        return remote(g_hbm.at[:, columns(1 - core)], g2.at[1], x_send.at[1], x_recv.at[1], partner, d)

    def slab_rows(b):
        return pl.ds(pl.multiple_of(b * slab, slab), slab)

    def up_copy(k):
        return remote(up_out.at[k], up_in.at[k], up_send.at[k], up_recv.at[k], s, d + 1)

    def dn_copy(k):
        return remote(dn_out.at[k], dn_in.at[k], dn_send.at[k], dn_recv.at[k], s, d - 1)

    def chain(k):
        back = dp - 1 - d

        @pl.when(d <= k)
        def _():
            b = dp - 1 - k + d

            @pl.when(d == 0)
            def _():
                up_out[k] = p_s[slab_rows(b), :].astype(BF16)

            if k:
                @pl.when(d > 0)
                def _():
                    up_copy(k - 1).wait_recv()
                    up_out[k] = (p_s[slab_rows(b), :] + up_in[k - 1].astype(F32)).astype(BF16)

            up_copy(k).start()

        @pl.when(back <= k)
        def _():
            b = k - back

            @pl.when(back == 0)
            def _():
                dn_out[k] = p_s[slab_rows(b), :].astype(BF16)

            if k:
                @pl.when(back > 0)
                def _():
                    dn_copy(k - 1).wait_recv()
                    dn_out[k] = (p_s[slab_rows(b), :] + dn_in[k - 1].astype(F32)).astype(BF16)

            dn_copy(k).start()

    def chain_drain():
        for k in range(dp - 1):
            pl.when(d <= k)(lambda: up_copy(k).wait_send())
            pl.when(dp - 1 - d <= k)(lambda: dn_copy(k).wait_send())

    def rs_copy(target, source):
        return remote(rs_out.at[target], rs_in.at[source], rs_send.at[target], rs_recv.at[source], 2 * target + core, d)

    def scatter():
        acc_s[...] = p_s[slab_rows(d), :]

        @pl.when(d > 0)
        def _():
            up_copy(dp - 2).wait_recv()
            acc_s[...] += up_in[dp - 2].astype(F32)

        @pl.when(d < dp - 1)
        def _():
            dn_copy(dp - 2).wait_recv()
            acc_s[...] += dn_in[dp - 2].astype(F32)

        for index in range(chips):
            rs_out[index] = acc_s[index * share : (index + 1) * share, :].astype(BF16)
        for step in range(1, chips):
            rs_copy(lax.rem(chip + step, chips), chip).start()

    def direct(step):
        return remote(total_s, spread.at[s], t_send.at[step], t_recv.at[s], lax.rem(s + 2 * step, seq), d)

    def forward(step):
        source = lax.rem(s + seq - 2 * step, seq)
        return remote(
            total_s if step == 0 else spread.at[source], spread.at[source],
            f_send.at[step], t_recv.at[source], partner, d,
        )

    def arrived(source):
        remote(total_s, spread.at[source], f_send.at[0], t_recv.at[source], partner, d).wait_recv()

    own_total = pltpu.make_async_copy(total_s, spread.at[s], own_sem.at[3, 0])

    def combine():
        value = rs_out[chip].astype(F32)
        for step in range(1, chips):
            source = lax.rem(chip + chips - step, chips)
            rs_copy(source, source).wait_recv()
            value = value + rs_in[source].astype(F32)
        total_s[...] = value.astype(BF16)
        for step in range(1, chips):
            direct(step).start()
        forward(0).start()
        own_total.start()

    def soften(h, index):
        cut = slice(index * block, (index + 1) * block)
        scores = lax.dot_general(k_s[h], q_s[h, cut, :], LAST, preferred_element_type=F32)
        top = jnp.max(scores, axis=0, keepdims=True)
        exps = jnp.exp2((scores - top) * to_log2)
        inv_s[h, :, cut] = 1.0 / jnp.sum(exps, axis=0, keepdims=True)
        e_s[h, :, cut] = exps.astype(BF16)

    def unpack(h):
        await_all(q_copy, own_q, h)
        for source in range(seq):
            cut = slice(source * rows, (source + 1) * rows)
            q_s[h, cut, :] = pack_in[h, source, :, 0:HEAD_DIM]
            k_s[h, cut, :] = pack_in[h, source, :, HEAD_DIM : 2 * HEAD_DIM]
            v_s[h, cut, 0:HEAD_DIM] = pack_in[h, source, :, 2 * HEAD_DIM : 3 * HEAD_DIM]
            v_s[h, cut, HEAD_DIM:AUG] = jnp.ones((rows, AUG - HEAD_DIM), BF16)

    def prepare(h):
        await_all(do_copy, own_do, h)
        for index in range(blocks):
            cut = slice(index * block, (index + 1) * block)
            column = jnp.broadcast_to(inv_s[h, :, cut], (8, block)).T[:, 0:1]
            qs_s[cut, :] = (q_s[h, cut, :].astype(F32) * (column * scale)).astype(BF16)
        for source in range(seq):
            cut = slice(source * rows, (source + 1) * rows)
            dos_s[cut, :] = do_in[h, source]
        dqt_s[...] = jnp.zeros_like(dqt_s)

    def differentiate(h, index):
        cut = slice(index * block, (index + 1) * block)
        d_out = dos_s[...]
        exps = e_s[h, cut, :]
        inverse = inv_s[h]
        d_probs = lax.dot_general(v_s[h, cut, :], d_out, LAST, preferred_element_type=F32)
        d_scores = (exps.astype(F32) * d_probs).astype(BF16)
        probs = (exps.astype(F32) * inverse).astype(BF16)
        d_v = jnp.dot(probs, d_out, preferred_element_type=F32)
        d_k = jnp.dot(d_scores, qs_s[...], preferred_element_type=F32)
        dqt_s[...] += lax.dot_general(k_s[h, cut, :], d_scores, FIRST, preferred_element_type=F32)
        grad_s[h, cut, HEAD_DIM : 2 * HEAD_DIM] = d_k.astype(BF16)
        grad_s[h, cut, 2 * HEAD_DIM : 3 * HEAD_DIM] = d_v[:, 0:HEAD_DIM].astype(BF16)

    def finish(h):
        grad_s[h, :, 0:HEAD_DIM] = (dqt_s[...] * (inv_s[h] * scale)).T.astype(BF16)
        send_all(grad_copy, own_grad, h)

    pl.semaphore_wait(barrier, seq + dp - 2)
    w_own(0)
    a_swap().start()
    g_swap().start()
    for copy in loads[:3]:
        copy.wait()
    for h in range(heads):
        pack(h)
        send_all(q_copy, own_q, h)
    for copy in loads[3:]:
        copy.wait()
    a_swap().wait_recv()
    g_swap().wait_recv()
    p_s[...] = factor * lax.dot_general(
        a2[...].reshape(2 * rows, features), g2[...].reshape(2 * rows, half), FIRST, preferred_element_type=F32
    )
    w_relay(0, 1)
    for h in range(1, heads):
        w_own(h)
    chain(0)

    links = 1
    for h in range(heads):
        unpack(h)
        for index in range(blocks):
            soften(h, index)
            if h == 0 and index == 0:
                for dist in range(2, dp - 1):
                    w_relay(0, dist)
            if h == 0 and index == blocks - 1:
                if dp > 2:
                    w_relay(0, dp - 1)
                w_finish(0)
                make_d_out(0)
                send_all(do_copy, own_do, 0)
                for g in range(1, heads):
                    w_relay(g, 1)
            if h == 1 and index == 0:
                for g in range(1, heads):
                    for dist in range(2, dp - 1):
                        w_relay(g, dist)
                if links < dp - 1:
                    chain(links)
                    links += 1

    for h in range(heads):
        prepare(h)
        for index in range(blocks):
            differentiate(h, index)
            if h == 0 and index == 0:
                for g in range(1, heads):
                    if dp > 2:
                        w_relay(g, dp - 1)
                    w_finish(g)
                    make_d_out(g)
                    send_all(do_copy, own_do, g)
        finish(h)
        if h == 0:
            while links < dp - 1:
                chain(links)
                links += 1

    scatter()
    combine()
    for step in range(1, chips):
        arrived(lax.rem(s + seq - 2 * step, seq))
        forward(step).start()
    for h in range(heads):
        await_all(grad_copy, own_grad, h)
    for step in range(chips):
        arrived(lax.rem(partner + seq - 2 * step, seq))
    own_total.wait()

    for h in range(heads):
        w_drain(h)
        drain_all(q_copy, h)
        drain_all(do_copy, h)
        drain_all(grad_copy, h)
    a_swap().wait_send()
    g_swap().wait_send()
    chain_drain()
    for step in range(1, chips):
        rs_copy(lax.rem(chip + step, chips), chip).wait_send()
        direct(step).wait_send()
    for step in range(chips):
        forward(step).wait_send()


def attention(seq, dp, factor, query, keys, values, attn, grad_y, w_rows):
    rows, features = query.shape
    heads = w_rows.shape[1]
    ratio = w_rows.shape[0]
    total = seq * rows
    half = features // 2
    slab = features // dp
    chips = seq // 2
    share = slab // chips
    block = 768
    while total % block or total * block > 1536 * 768:
        block //= 2
    dma = pltpu.SemaphoreType.DMA
    hbm = pl.BlockSpec(memory_space=pl.ANY)
    low = lambda *shape: pltpu.VMEM(shape, BF16)
    wide = lambda *shape: pltpu.VMEM(shape, F32)
    links = max(dp - 1, 1)
    return pl.pallas_call(
        functools.partial(attention_kernel, seq, dp, heads, block, factor),
        out_shape=(
            jax.ShapeDtypeStruct((heads, seq, rows, 3 * HEAD_DIM), BF16),
            jax.ShapeDtypeStruct((seq, share, half), BF16),
        ),
        in_specs=[hbm] * 6,
        out_specs=(hbm, hbm),
        scratch_shapes=[
            low(rows, features), low(rows, features), low(rows, features), low(rows, features),
            low(2, rows, features), low(2, rows, half),
            low(heads, seq, HEAD_DIM, features),
            low(heads, seq, rows, 3 * HEAD_DIM), low(heads, seq, rows, 3 * HEAD_DIM),
            low(heads, seq, rows, AUG), low(heads, seq, rows, AUG),
            low(heads, total, HEAD_DIM), low(heads, total, HEAD_DIM), low(heads, total, AUG),
            low(total, HEAD_DIM), low(total, AUG),
            low(heads, total, total), wide(heads, 1, total),
            wide(HEAD_DIM, total), low(heads, total, 3 * HEAD_DIM),
            wide(features, half),
            low(links, slab, half), low(links, slab, half), low(links, slab, half), low(links, slab, half),
            wide(slab, half), low(chips, share, half), low(chips, share, half), low(share, half),
            dma((6 + heads,)), dma((4, heads)),
            dma((heads, dp)), dma((heads, dp)), dma((heads, dp)), dma((heads, dp, 2)),
            dma((2,)), dma((2,)),
            dma((heads, seq)), dma((heads, seq)), dma((heads, seq)), dma((heads, seq)),
            dma((heads, seq)), dma((heads, seq)),
            dma((links,)), dma((links,)), dma((links,)), dma((links,)),
            dma((chips,)), dma((chips,)), dma((chips,)), dma((chips,)), dma((seq,)),
        ],
        compiler_params=pltpu.CompilerParams(
            collective_id=0, has_side_effects=True, vmem_limit_bytes=VMEM_LIMIT
        ),
        name="attention_backward",
    )(query, keys, values, attn, grad_y, w_rows)


def unpack_kernel(landed, spread, dq_ref, dk_ref, dv_ref, out_ref):
    heads, seq = landed.shape[:2]
    share, half = spread.shape[1:]
    width = heads * HEAD_DIM
    for source in range(seq):
        for h in range(heads):
            start = source * width + h * HEAD_DIM
            for index, ref in enumerate((dq_ref, dk_ref, dv_ref)):
                ref[:, start : start + HEAD_DIM] = landed[
                    h, source, :, index * HEAD_DIM : (index + 1) * HEAD_DIM
                ]
        top = (source // 2) * share
        side = (source % 2) * half
        out_ref[top : top + share, side : side + half] = spread[source].astype(F32)


def unpack(dp, landed, spread):
    rows = landed.shape[2]
    features = landed.shape[0] * landed.shape[1] * HEAD_DIM
    vmem = pl.BlockSpec(memory_space=pltpu.VMEM)
    block = jax.ShapeDtypeStruct((rows, features), BF16)
    return pl.pallas_call(
        unpack_kernel,
        out_shape=(block, block, block, jax.ShapeDtypeStruct((features // dp, features), F32)),
        in_specs=[vmem] * 2,
        out_specs=(vmem,) * 4,
        compiler_params=pltpu.CompilerParams(vmem_limit_bytes=VMEM_LIMIT),
        name="unpack",
    )(landed, spread)


def body(query, keys, values, attn, d_block, w_out):
    seq = lax.axis_size("seq")
    dp = lax.axis_size("dp")
    rows, features = query.shape[1:]
    heads = features // HEAD_DIM // seq
    flat = lambda array: array.reshape(rows, features)
    factor = 1.0 / float(dp * rows * seq) ** 0.5
    landed, spread = attention(
        seq, dp, factor, flat(query), flat(keys), flat(values), flat(attn), flat(d_block),
        w_out.reshape(seq // dp, heads, HEAD_DIM, features),
    )
    d_query, d_keys, d_values, d_weight = unpack(dp, landed, spread)
    whole = lambda array: array.reshape(1, rows, features)
    return whole(d_query), whole(d_keys), whole(d_values), d_weight


def solution(mesh):
    blocks = P("dp", "seq", None)
    return jax.shard_map(
        body,
        mesh=mesh,
        in_specs=(blocks,) * 5 + (P("dp", None),),
        out_specs=(blocks, blocks, blocks, P("dp", None)),
        check_vma=False,
    )
```

time: 96.2 us -> 84 us (0.87)
  Pallas kernels: 95.4 us -> 83.2 us
    pallas_call x2 -> x1, Pallas kernels: 91.1 us -> 78.8 us  [attention(): pl.pallas_call(functools.partial(attention_kernel, seq, dp, heads, block,...]
where the time goes in v1:
time: 84 us; the launch traced here: 83.8 us
  Pallas kernels  83.2 us (99%)
    pallas_call x1, Pallas kernels, attention(): pl.pallas_call(functools.partial(attention_kernel, seq, dp, heads, block,...  78.8 us
    pallas_call x1, Pallas kernels, unpack(): pl.pallas_call(unpack_kernel, out_shape=(block, block, block, jax.ShapeDt...  4.35 us

profile of v1, /device:TPU:1, one launch (start us, length us, event | category | flops | bytes accessed | tf_op | source)
XLA Modules:
  0.0 83.8 jit_solution(1836977900661067746)
XLA Ops:
  0.6 78.8 %attention_backward.1 = (bf16[2,8,192,240]{3,2,1,0:T(8,128)(2,1)}, bf16[8,80,640]{2,1,0:T(8,128)(2,1)}) custom-call(bf16[192,1280]{1,0:T(8,128)(2,1)} %bitcast.10, bf16[192,1280]{1,0:T(8,128)(2,1)} %bitcast.11, bf16[192,1280]{1,0:T(8,128)(2,1)} %bitcast.12, bf16[192,1280]{1,0:T(8,128)(2,1)} %bitcast.13, bf16[192,1280]{1,0:T(8,128)(2,1)} %bitcast.14, ...), custom_call_target="tpu_custom_call" | custom-call | tf_op jit(solution)/shard_map/attention_backward/pallas_call | solution.py:448
  79.5 4.4 %unpack.1 = (bf16[192,1280]{1,0:T(8,128)(2,1)}, bf16[192,1280]{1,0:T(8,128)(2,1)}, bf16[192,1280]{1,0:T(8,128)(2,1)}, f32[320,1280]{1,0:T(8,128)}) custom-call(bf16[2,8,192,240]{3,2,1,0:T(8,128)(2,1)} %get-tuple-element.10.landed, bf16[8,80,640]{2,1,0:T(8,128)(2,1)} %get-tuple-element.11.spread), custom_call_target="tpu_custom_call" | custom-call | tf_op jit(solution)/shard_map/unpack/pallas_call | solution.py:505

commit v2 on v1

--- a/solution.py
+++ b/solution.py
@@ -9,7 +9,9 @@
 from jax.sharding import PartitionSpec as P
 
 HEAD_DIM = 80
-AUG = HEAD_DIM + 8
+AUG = HEAD_DIM + 3
+FOLD = 3
+PIECES = 2
 MESH = pl.DeviceIdType.MESH
 VMEM_LIMIT = 62 * 1024 * 1024
 LAST = (((1,), (1,)), ((), ()))
@@ -21,7 +23,7 @@
 def attention_kernel(
     seq, dp, heads, block, factor,
     q_hbm, k_hbm, v_hbm, a_hbm, g_hbm, w_hbm, landed, spread,
-    q_v, k_v, v_v, g_v, a2, g2, w_all, packed, pack_in, do_out, do_in,
+    q_v, k_v, v_v, g_v, a2, g2, w_all, packed, pack_in, a_s, do_out, do_in,
     q_s, k_s, v_s, qs_s, dos_s, e_s, inv_s, dqt_s, grad_s,
     p_s, up_out, up_in, dn_out, dn_in, acc_s, rs_out, rs_in, total_s,
     in_sem, own_sem, wu_send, wd_send, wp_send, w_recv, x_send, x_recv,
@@ -96,6 +98,16 @@
         pl.when(d < dp - 1)(lambda: w_up(h, d, True).start())
         pl.when(d > 0)(lambda: w_down(h, d, True).start())
 
+    def w_ends(h):
+        pl.when(d == 0)(lambda: w_up(h, d, True).start())
+        pl.when(d == dp - 1)(lambda: w_down(h, d, True).start())
+
+    def w_inner(h):
+        @pl.when((d > 0) & (d < dp - 1))
+        def _():
+            w_up(h, d, True).start()
+            w_down(h, d, True).start()
+
     def w_relay(h, dist):
         @pl.when(d >= dist)
         def _():
@@ -110,12 +122,6 @@
             w_side(h, b, core).wait_recv()
             pl.when(d > 0)(lambda: w_down(h, b, False).start())
             w_side(h, b, core).start()
-
-    def w_finish(h):
-        for dist in range(1, dp):
-            pl.when(d >= dist)(lambda: w_side(h, d - dist, 1 - core).wait_recv())
-            pl.when(d + dist < dp)(lambda: w_side(h, d + dist, 1 - core).wait_recv())
-        own_w[h].wait()
 
     def w_drain(h):
         pl.when(d < dp - 1)(lambda: w_up(h, d, True).wait_send())
@@ -174,22 +180,45 @@
             for index, ref in enumerate((q_v, k_v, v_v)):
                 packed[h, peer, :, index * HEAD_DIM : (index + 1) * HEAD_DIM] = ref[:, low : low + HEAD_DIM]
 
-    def make_d_out(h):
+    def pack_attn(h):
+        for peer in range(seq):
+            low = peer * width + h * HEAD_DIM
+            a_s[h, peer] = a2[0, :, low : low + HEAD_DIM]
+
+    def make_d_out(h, b):
         d_out = lax.dot_general(
-            g_v[...], w_all[h].reshape(seq * HEAD_DIM, features), LAST, preferred_element_type=F32
+            g_v[...], w_all[h, pl.ds(b * ratio, ratio)].reshape(ratio * HEAD_DIM, features), LAST,
+            preferred_element_type=F32,
         ).astype(BF16)
         lane = lax.broadcasted_iota(jnp.int32, (rows, AUG - HEAD_DIM), 1)
-        for peer in range(seq):
-            low = peer * width + h * HEAD_DIM
-            piece = d_out[:, peer * HEAD_DIM : (peer + 1) * HEAD_DIM]
-            product = piece.astype(F32) * a2[0, :, low : low + HEAD_DIM].astype(F32)
+        fold = rows // FOLD
+        for member in range(ratio):
+            peer = b * ratio + member
+            piece = d_out[:, member * HEAD_DIM : (member + 1) * HEAD_DIM]
+            product = piece.astype(F32) * a_s[h, peer].astype(F32)
             minus = -jnp.sum(product, axis=1, keepdims=True)
             first = minus.astype(BF16).astype(F32)
             second = (minus - first).astype(BF16).astype(F32)
             third = minus - first - second
-            tail = jnp.where(lane == 0, first, jnp.where(lane == 1, second, jnp.where(lane == 2, third, 0.0)))
-            do_out[h, peer, :, 0:HEAD_DIM] = piece
-            do_out[h, peer, :, HEAD_DIM:AUG] = tail.astype(BF16)
+            tail = jnp.where(lane == 0, first, jnp.where(lane == 1, second, third)).astype(BF16)
+            for index in range(FOLD):
+                cut = slice(index * fold, (index + 1) * fold)
+                do_out[h, peer, :, index * AUG : index * AUG + HEAD_DIM] = piece[cut]
+                do_out[h, peer, :, index * AUG + HEAD_DIM : (index + 1) * AUG] = tail[cut]
+        for member in range(ratio):
+            peer = b * ratio + member
+            pl.when(peer != s)(lambda: do_copy(h, peer, s).start())
+            pl.when(peer == s)(lambda: own_do(h).start())
+
+    def d_out_pair(h, dist):
+        @pl.loop(0, 2)
+        def _(side):
+            b = d + (2 * side - 1) * dist
+
+            @pl.when((b >= 0) & (b < dp))
+            def _():
+                w_side(h, b, 1 - core).wait_recv()
+                make_d_out(h, b)
 
     def a_swap():
         return remote(a_hbm, a2.at[1], x_send.at[0], x_recv.at[0], partner, d)
@@ -197,70 +226,69 @@
     def g_swap():
         return remote(g_hbm.at[:, columns(1 - core)], g2.at[1], x_send.at[1], x_recv.at[1], partner, d)
 
-    def slab_rows(b):
-        return pl.ds(pl.multiple_of(b * slab, slab), slab)
-
-    def up_copy(k):
-        return remote(up_out.at[k], up_in.at[k], up_send.at[k], up_recv.at[k], s, d + 1)
-
-    def dn_copy(k):
-        return remote(dn_out.at[k], dn_in.at[k], dn_send.at[k], dn_recv.at[k], s, d - 1)
-
-    def chain(k):
-        back = dp - 1 - d
-
-        @pl.when(d <= k)
-        def _():
-            b = dp - 1 - k + d
-
-            @pl.when(d == 0)
-            def _():
-                up_out[k] = p_s[slab_rows(b), :].astype(BF16)
-
-            if k:
-                @pl.when(d > 0)
-                def _():
-                    up_copy(k - 1).wait_recv()
-                    up_out[k] = (p_s[slab_rows(b), :] + up_in[k - 1].astype(F32)).astype(BF16)
-
-            up_copy(k).start()
-
-        @pl.when(back <= k)
-        def _():
-            b = k - back
-
-            @pl.when(back == 0)
-            def _():
-                dn_out[k] = p_s[slab_rows(b), :].astype(BF16)
-
-            if k:
-                @pl.when(back > 0)
-                def _():
-                    dn_copy(k - 1).wait_recv()
-                    dn_out[k] = (p_s[slab_rows(b), :] + dn_in[k - 1].astype(F32)).astype(BF16)
-
-            dn_copy(k).start()
+    def slab_rows(b, j):
+        return pl.ds(pl.multiple_of(b * slab + j * (slab // PIECES), 8), slab // PIECES)
+
+    def up_copy(k, j):
+        return remote(up_out.at[k, j], up_in.at[k, j], up_send.at[k, j], up_recv.at[k, j], s, d + 1)
+
+    def dn_copy(k, j):
+        return remote(dn_out.at[k, j], dn_in.at[k, j], dn_send.at[k, j], dn_recv.at[k, j], s, d - 1)
+
+    back = dp - 1 - d
+
+    def chain_ends():
+        @pl.when(d == 0)
+        def _():
+            for k in range(dp - 1):
+                for j in range(PIECES):
+                    up_out[k, j] = p_s[slab_rows(dp - 1 - k, j), :].astype(BF16)
+                    up_copy(k, j).start()
+
+        @pl.when(back == 0)
+        def _():
+            for k in range(dp - 1):
+                for j in range(PIECES):
+                    dn_out[k, j] = p_s[slab_rows(k, j), :].astype(BF16)
+                    dn_copy(k, j).start()
+
+    def chain(k, j):
+        @pl.when((d > 0) & (d <= k))
+        def _():
+            up_copy(k - 1, j).wait_recv()
+            up_out[k, j] = (p_s[slab_rows(dp - 1 - k + d, j), :] + up_in[k - 1, j].astype(F32)).astype(BF16)
+            up_copy(k, j).start()
+
+        @pl.when((back > 0) & (back <= k))
+        def _():
+            dn_copy(k - 1, j).wait_recv()
+            dn_out[k, j] = (p_s[slab_rows(k - back, j), :] + dn_in[k - 1, j].astype(F32)).astype(BF16)
+            dn_copy(k, j).start()
 
     def chain_drain():
         for k in range(dp - 1):
-            pl.when(d <= k)(lambda: up_copy(k).wait_send())
-            pl.when(dp - 1 - d <= k)(lambda: dn_copy(k).wait_send())
+            for j in range(PIECES):
+                pl.when(d <= k)(lambda: up_copy(k, j).wait_send())
+                pl.when(back <= k)(lambda: dn_copy(k, j).wait_send())
 
     def rs_copy(target, source):
         return remote(rs_out.at[target], rs_in.at[source], rs_send.at[target], rs_recv.at[source], 2 * target + core, d)
 
     def scatter():
-        acc_s[...] = p_s[slab_rows(d), :]
-
-        @pl.when(d > 0)
-        def _():
-            up_copy(dp - 2).wait_recv()
-            acc_s[...] += up_in[dp - 2].astype(F32)
-
-        @pl.when(d < dp - 1)
-        def _():
-            dn_copy(dp - 2).wait_recv()
-            acc_s[...] += dn_in[dp - 2].astype(F32)
+        tall = slab // PIECES
+        for j in range(PIECES):
+            cut = slice(j * tall, (j + 1) * tall)
+            acc_s[cut, :] = p_s[slab_rows(d, j), :]
+
+            @pl.when(d > 0)
+            def _():
+                up_copy(dp - 2, j).wait_recv()
+                acc_s[cut, :] += up_in[dp - 2, j].astype(F32)
+
+            @pl.when(d < dp - 1)
+            def _():
+                dn_copy(dp - 2, j).wait_recv()
+                acc_s[cut, :] += dn_in[dp - 2, j].astype(F32)
 
         for index in range(chips):
             rs_out[index] = acc_s[index * share : (index + 1) * share, :].astype(BF16)
@@ -317,9 +345,11 @@
             cut = slice(index * block, (index + 1) * block)
             column = jnp.broadcast_to(inv_s[h, :, cut], (8, block)).T[:, 0:1]
             qs_s[cut, :] = (q_s[h, cut, :].astype(F32) * (column * scale)).astype(BF16)
+        fold = rows // FOLD
         for source in range(seq):
-            cut = slice(source * rows, (source + 1) * rows)
-            dos_s[cut, :] = do_in[h, source]
+            for index in range(FOLD):
+                start = source * rows + index * fold
+                dos_s[start : start + fold, :] = do_in[h, source, :, index * AUG : (index + 1) * AUG]
         dqt_s[...] = jnp.zeros_like(dqt_s)
 
     def differentiate(h, index):
@@ -338,10 +368,11 @@
 
     def finish(h):
         grad_s[h, :, 0:HEAD_DIM] = (dqt_s[...] * (inv_s[h] * scale)).T.astype(BF16)
-        send_all(grad_copy, own_grad, h)
 
     pl.semaphore_wait(barrier, seq + dp - 2)
     w_own(0)
+    for g in range(1, heads):
+        w_ends(g)
     a_swap().start()
     g_swap().start()
     for copy in loads[:3]:
@@ -351,59 +382,83 @@
         send_all(q_copy, own_q, h)
     for copy in loads[3:]:
         copy.wait()
+    for h in range(heads):
+        pack_attn(h)
+    own_w[0].wait()
+    make_d_out(0, d)
     a_swap().wait_recv()
     g_swap().wait_recv()
     p_s[...] = factor * lax.dot_general(
         a2[...].reshape(2 * rows, features), g2[...].reshape(2 * rows, half), FIRST, preferred_element_type=F32
     )
-    w_relay(0, 1)
-    for h in range(1, heads):
-        w_own(h)
-    chain(0)
-
-    links = 1
+    chain_ends()
+    for dist in range(1, dp - 1):
+        w_relay(0, dist)
+        if dist < dp - 2:
+            d_out_pair(0, dist)
+    for g in range(1, heads):
+        w_inner(g)
+    links = [(k, j) for k in range(1, dp - 1) for j in range(PIECES)]
+
+    def link():
+        if links:
+            chain(*links.pop(0))
+
     for h in range(heads):
         unpack(h)
         for index in range(blocks):
             soften(h, index)
             if h == 0 and index == 0:
-                for dist in range(2, dp - 1):
-                    w_relay(0, dist)
+                if dp > 2:
+                    d_out_pair(0, dp - 2)
+                for g in range(1, heads):
+                    own_w[g].wait()
+                    make_d_out(g, d)
             if h == 0 and index == blocks - 1:
+                w_relay(0, dp - 1)
+                d_out_pair(0, dp - 1)
+                for g in range(1, heads):
+                    if dp > 2:
+                        w_relay(g, 1)
+                link()
+            if h == 1 and index == 0:
                 if dp > 2:
-                    w_relay(0, dp - 1)
-                w_finish(0)
-                make_d_out(0)
-                send_all(do_copy, own_do, 0)
-                for g in range(1, heads):
-                    w_relay(g, 1)
-            if h == 1 and index == 0:
+                    for g in range(1, heads):
+                        d_out_pair(g, 1)
+                link()
+            if h == 1 and index == blocks - 1:
                 for g in range(1, heads):
                     for dist in range(2, dp - 1):
                         w_relay(g, dist)
-                if links < dp - 1:
-                    chain(links)
-                    links += 1
+                        d_out_pair(g, dist)
+                link()
 
     for h in range(heads):
         prepare(h)
+        last = h == heads - 1
         for index in range(blocks):
             differentiate(h, index)
-            if h == 0 and index == 0:
-                for g in range(1, heads):
-                    if dp > 2:
-                        w_relay(g, dp - 1)
-                    w_finish(g)
-                    make_d_out(g)
-                    send_all(do_copy, own_do, g)
+            if last and index == blocks - 2:
+                while links:
+                    link()
+                scatter()
         finish(h)
         if h == 0:
-            while links < dp - 1:
-                chain(links)
-                links += 1
-
-    scatter()
-    combine()
+            link()
+            for g in range(1, heads):
+                w_relay(g, dp - 1)
+                d_out_pair(g, dp - 1)
+        if not last:
+            send_all(grad_copy, own_grad, h)
+    if blocks == 1:
+        while links:
+            link()
+        scatter()
+    own_grad(heads - 1).start()
+    for step in range(1, seq):
+        grad_copy(heads - 1, lax.rem(s + step, seq), s).start()
+        if step == seq - 1:
+            combine()
     for step in range(1, chips):
         arrived(lax.rem(s + seq - 2 * step, seq))
         forward(step).start()
@@ -458,20 +513,20 @@
             low(2, rows, features), low(2, rows, half),
             low(heads, seq, HEAD_DIM, features),
             low(heads, seq, rows, 3 * HEAD_DIM), low(heads, seq, rows, 3 * HEAD_DIM),
-            low(heads, seq, rows, AUG), low(heads, seq, rows, AUG),
+            low(heads, seq, rows, HEAD_DIM), low(heads, seq, rows // FOLD, FOLD * AUG), low(heads, seq, rows // FOLD, FOLD * AUG),
             low(heads, total, HEAD_DIM), low(heads, total, HEAD_DIM), low(heads, total, AUG),
             low(total, HEAD_DIM), low(total, AUG),
             low(heads, total, total), wide(heads, 1, total),
             wide(HEAD_DIM, total), low(heads, total, 3 * HEAD_DIM),
             wide(features, half),
-            low(links, slab, half), low(links, slab, half), low(links, slab, half), low(links, slab, half),
+            *[low(links, PIECES, slab // PIECES, half)] * 4,
             wide(slab, half), low(chips, share, half), low(chips, share, half), low(share, half),
             dma((6 + heads,)), dma((4, heads)),
             dma((heads, dp)), dma((heads, dp)), dma((heads, dp)), dma((heads, dp, 2)),
             dma((2,)), dma((2,)),
             dma((heads, seq)), dma((heads, seq)), dma((heads, seq)), dma((heads, seq)),
             dma((heads, seq)), dma((heads, seq)),
-            dma((links,)), dma((links,)), dma((links,)), dma((links,)),
+            *[dma((links, PIECES))] * 4,
             dma((chips,)), dma((chips,)), dma((chips,)), dma((chips,)), dma((seq,)),
         ],
         compiler_params=pltpu.CompilerParams(

time: 84 us -> 77.9 us (0.927); the launches traced: 83.8 us -> 76.7 us
  Pallas kernels: 83.2 us -> 76.1 us
    pallas_call x1, Pallas kernels: 78.8 us -> 71.7 us  [attention(): pl.pallas_call(functools.partial(attention_kernel, seq, dp, heads, block,...]
where the time goes in v2:
time: 77.9 us; the launch traced here: 76.7 us
  Pallas kernels  76.1 us (98%)
    pallas_call x1, Pallas kernels, attention(): pl.pallas_call(functools.partial(attention_kernel, seq, dp, heads, block,...  71.7 us
    pallas_call x1, Pallas kernels, unpack(): pl.pallas_call(unpack_kernel, out_shape=(block, block, block, jax.ShapeDt...  4.35 us

profile of v2, /device:TPU:1, one launch (start us, length us, event | category | flops | bytes accessed | tf_op | source)
XLA Modules:
  0.0 76.7 jit_solution(10112540626640165616)
XLA Ops:
  0.6 71.7 %attention_backward.1 = (bf16[2,8,192,240]{3,2,1,0:T(8,128)(2,1)}, bf16[8,80,640]{2,1,0:T(8,128)(2,1)}) custom-call(bf16[192,1280]{1,0:T(8,128)(2,1)} %bitcast.10, bf16[192,1280]{1,0:T(8,128)(2,1)} %bitcast.11, bf16[192,1280]{1,0:T(8,128)(2,1)} %bitcast.12, bf16[192,1280]{1,0:T(8,128)(2,1)} %bitcast.13, bf16[192,1280]{1,0:T(8,128)(2,1)} %bitcast.14, ...), custom_call_target="tpu_custom_call" | custom-call | tf_op jit(solution)/shard_map/attention_backward/pallas_call | solution.py:503
  72.4 4.4 %unpack.1 = (bf16[192,1280]{1,0:T(8,128)(2,1)}, bf16[192,1280]{1,0:T(8,128)(2,1)}, bf16[192,1280]{1,0:T(8,128)(2,1)}, f32[320,1280]{1,0:T(8,128)}) custom-call(bf16[2,8,192,240]{3,2,1,0:T(8,128)(2,1)} %get-tuple-element.10.landed, bf16[8,80,640]{2,1,0:T(8,128)(2,1)} %get-tuple-element.11.spread), custom_call_target="tpu_custom_call" | custom-call | tf_op jit(solution)/shard_map/unpack/pallas_call | solution.py:560
